TPU v7x, 256 devices: a whole 4x4x8 slice. The times are simulated.
256 devices in a mesh: pulse: 16 (over z, core), range: 16 (over x, y).
Axes of the slice: x: 4, y: 4, z: 8, core: 2. Of those that a mesh axis runs over, the one named last changes fastest.
Arguments:
- pulse_data: bfloat16 [2, 16384, 4096], P(None, 'pulse', 'range'), may hold values from -6 to 6
- merge_taps: int32 [3, 2, 4, 16384], P(None, None, None, 'pulse'), may hold values from 0 to 1023, as said below
- merge_weights: bfloat16 [3, 2, 4, 16384], P(None, None, None, 'pulse'), may hold values from -2 to 2
- squint: float32 [3, 16384], P(None, 'pulse'), may hold values from -8 to 8
Outputs:
- focused: float32 [2, 1024, 4096], P(None, 'pulse', 'range')
Inputs may be any that keep to these rules, and one draw needn't show every extreme that they name: `merge_taps`: for each level, source half and output beam, the 4 taps name different beams of the source block.
All inputs are finite; a program needn't handle non-finite values.
Results may differ from a plain program's by a relative error of at most 0.0064.
Values may be sent and summed in bfloat16 or wider, within the bound.
A program may use at most 64 MiB of HBM per device.

v0:
```python
import math

import jax
import jax.numpy as jnp
from jax import lax
from jax.experimental import pallas as pl
from jax.experimental.pallas import tpu as pltpu
from jax.sharding import PartitionSpec as P

RANGES = 4096
ANGLES = 16384
BEAMS = 1024
COLS = 256
BLOCK = 64
EPSILON = 1e-06
TWO_PI = 2.0 * math.pi
RANGE_STEP = TWO_PI / RANGES
MESH = pl.DeviceIdType.MESH
f32 = jnp.float32
bf16 = jnp.bfloat16
NT = (((1,), (1,)), ((), ()))


def flipped(index, bit):
    return index + bit - 2 * bit * ((index // bit) % 2)


def kernel(
    data, taps, weights, squint, out,
    dT, prm, snd, W, rowid, rb, rs, S1, U, X, Y, us, tab,
    fst, psn, prx, zsn, zrx, G, F, cx, cy,
    part_s, part_r, prm_s, prm_r, pair_s, pair_r, z_s, z_r, x_s, x_r, y_s, y_r,
):
    pulse = lax.axis_index("pulse")
    ranged = lax.axis_index("range")
    z = pulse // 2
    core = pulse % 2
    gx = ranged // 4
    gy = ranged % 4
    other = 1 - core
    buddy = flipped(pulse, 1)
    q2 = flipped(pulse, 2)
    q4 = flipped(pulse, 4)
    q6 = flipped(q2, 4)

    def z_peer(k):
        return ((z + k) % 8) * 2 + core

    def x_peer(k):
        return ((gx + k) % 4) * 4 + gy

    def y_peer(k):
        return gx * 4 + (gy + k) % 4

    barrier = pltpu.get_barrier_semaphore()
    pl.semaphore_signal(barrier, inc=1, device_id={"pulse": buddy}, device_id_type=MESH)
    for k in range(1, 8):
        pl.semaphore_signal(barrier, inc=1, device_id={"pulse": z_peer(k)}, device_id_type=MESH)
    for k in range(1, 4):
        pl.semaphore_signal(barrier, inc=1, device_id={"range": x_peer(k)}, device_id_type=MESH)
        pl.semaphore_signal(barrier, inc=1, device_id={"range": y_peer(k)}, device_id_type=MESH)

    for t in range(2):
        dT[0, t * COLS:(t + 1) * COLS, :] = data[t].T

    def fill(ref, level, source):
        ref[0:4, :] = taps[level, source].astype(f32)
        ref[4:8, :] = weights[level, source].astype(f32)
        ref[8:9, :] = squint[level:level + 1, :]

    fill(snd.at[0], 1, 1)
    fill(snd.at[1], 2, 1)
    fill(prm.at[4], 2, 0)

    pl.semaphore_wait(barrier, 14)

    part = pltpu.make_async_remote_copy(
        dT.at[0], dT.at[1], part_s, part_r, device_id={"pulse": buddy}, device_id_type=MESH)
    part.start()
    prm_copies = []
    for n, (src, slot, target) in enumerate((
        (snd.at[1], 7, q6), (snd.at[1], 5, q4), (snd.at[0], 3, q2), (prm.at[4], 6, q2))):
        copy = pltpu.make_async_remote_copy(
            src, prm.at[slot], prm_s.at[n], prm_r.at[n],
            device_id={"pulse": target}, device_id_type=MESH)
        copy.start()
        prm_copies.append(copy)

    fill(prm.at[0], 0, 0)
    fill(prm.at[1], 0, 1)
    fill(prm.at[2], 1, 0)

    rowid[...] = lax.broadcasted_iota(jnp.int32, (256, 256), 0).astype(f32).astype(bf16)

    def build(m):
        def tile(step, carry):
            nt = step // 4
            kb = step % 4
            cols = pl.ds(pl.multiple_of(nt * 256, 256), 256)
            base = (kb * 256).astype(f32)
            rows = rowid[...]
            val = jnp.zeros((256, 256), bf16)
            for tap in range(4):
                place = (prm[m, tap:tap + 1, cols] - base).astype(bf16)
                weight = prm[m, 4 + tap:5 + tap, cols].astype(bf16)
                val = jnp.where(rows == place, weight, val)
            W[m, nt, pl.ds(pl.multiple_of(kb * 256, 256), 256), :] = val
            return carry

        lax.fori_loop(0, 16, tile, 0)

    first_range = (ranged * COLS).astype(f32)

    def prepare_rotation(m):
        slope = prm[m, 8:9, :]
        i8 = lax.broadcasted_iota(jnp.int32, (8, BEAMS), 0).astype(f32)
        phase = slope * ((i8 + first_range) * RANGE_STEP)
        c0 = jnp.cos(phase)
        s0 = jnp.sin(phase)
        far = slope * (jnp.where(i8 < 1.0, 8.0, 128.0) * RANGE_STEP)
        cf = jnp.cos(far)
        sf = jnp.sin(far)
        rb[m, 0, 0] = c0
        rb[m, 0, 1] = s0
        ch = cf[1:2]
        sh = sf[1:2]
        rb[m, 1, 0] = c0 * ch - s0 * sh
        rb[m, 1, 1] = s0 * ch + c0 * sh
        rs[m, 0] = jnp.broadcast_to(cf[0:1], (8, BEAMS))
        rs[m, 1] = jnp.broadcast_to(sf[0:1], (8, BEAMS))

    def rotated(real, imag, m, half, cols):
        c = rb[m, half, 0, :, cols]
        s = rb[m, half, 1, :, cols]
        c8 = rs[m, 0, :, cols]
        s8 = rs[m, 1, :, cols]
        reals = []
        imags = []
        for i in range(real.shape[0] // 8):
            a = real[8 * i:8 * i + 8]
            b = imag[8 * i:8 * i + 8]
            reals.append(c * a - s * b)
            imags.append(s * a + c * b)
            c, s = c * c8 - s * s8, s * c8 + c * s8
        return jnp.concatenate(reals, axis=0), jnp.concatenate(imags, axis=0)

    for m in (0, 1, 2, 4):
        build(m)
        if m != 1:
            prepare_rotation(m)

    part.wait()

    def level0(nt, carry):
        cols = pl.ds(pl.multiple_of(nt * 256, 256), 256)
        acc = jnp.dot(dT[0], W[0, nt], preferred_element_type=f32)
        acc = acc + jnp.dot(dT[1], W[1, nt], preferred_element_type=f32)
        for half in range(2):
            re, im = rotated(
                acc[128 * half:128 * half + 128],
                acc[256 + 128 * half:256 + 128 * half + 128], 0, half, cols)
            S1[half, 0:128, cols] = re.astype(bf16)
            S1[half, 128:256, cols] = im.astype(bf16)
        return carry

    lax.fori_loop(0, 4, level0, 0)

    for copy in prm_copies:
        copy.wait()

    for m in (3, 5, 6, 7):
        build(m)
        prepare_rotation(m)

    angle = lax.broadcasted_iota(jnp.int32, (16, BEAMS), 1) + BEAMS * (core + 8 * (z // 4))
    up = lax.broadcasted_iota(jnp.int32, (16, BEAMS), 0)
    theta = ((64 * up * angle) % ANGLES).astype(f32) * (TWO_PI / ANGLES)
    us[0] = jnp.cos(theta)
    us[1] = jnp.sin(theta)

    def table(k, carry):
        a8 = lax.broadcasted_iota(jnp.int32, (8, BEAMS), 1) + BEAMS * (core + 8 * (z // 4))
        v8 = 8 * lax.broadcasted_iota(jnp.int32, (8, BEAMS), 0) + k
        small = ((v8 * a8) % ANGLES).astype(f32) * (TWO_PI / ANGLES)
        vc = jnp.cos(small)
        vs = jnp.sin(small)
        for pair in range(8):
            cs = []
            ss = []
            for u in (2 * pair, 2 * pair + 1):
                uc = us[0, u:u + 1, :]
                un = us[1, u:u + 1, :]
                cs.append(uc * vc - un * vs)
                ss.append(un * vc + uc * vs)
            tab[k, 16 * pair:16 * pair + 16, :] = jnp.concatenate(cs, axis=0).astype(bf16)
            tab[k, 128 + 16 * pair:144 + 16 * pair, :] = jnp.concatenate(ss, axis=0).astype(bf16)
        return carry

    lax.fori_loop(0, 8, table, 0)

    root = math.sqrt(0.5)

    def level1(half):
        def body(nt, carry):
            cols = pl.ds(pl.multiple_of(nt * 256, 256), 256)
            for j in range(2):
                acc = jnp.dot(S1[half], W[2 + j, nt], preferred_element_type=f32)
                re, im = rotated(acc[:128], acc[128:], 2 + j, half, cols)
                U[j, 0:128, cols] = re.astype(bf16)
                U[j, 128:256, cols] = im.astype(bf16)
            return carry

        lax.fori_loop(0, 4, body, 0)

    bit0 = z % 2
    bit1 = (z // 2) % 2

    def level2(half):
        def body(nt, carry):
            cols = pl.ds(pl.multiple_of(nt * 256, 256), 256)
            for i, m in enumerate((4, 6, 5, 7)):
                acc = jnp.dot(U[i % 2], W[m, nt], preferred_element_type=f32)
                re, im = rotated(acc[:128], acc[128:], m, half, cols)
                at0 = bit0 if i % 2 == 0 else 1 - bit0
                at1 = bit1 if i // 2 == 0 else 1 - bit1
                slot = at0 + 2 * at1
                X[slot, 0:128, :] = re
                X[slot, 128:256, :] = im

            def rows16(step, carry):
                top = pl.ds(pl.multiple_of(step * 16, 16), 16)
                low = pl.ds(pl.multiple_of(128 + step * 16, 16), 16)
                xr = [X[n, top, :] for n in range(4)]
                xi = [X[n, low, :] for n in range(4)]
                e = [
                    (xr[0] + xr[2], xi[0] + xi[2]),
                    (xr[0] + xi[2], xi[0] - xr[2]),
                    (xr[0] - xr[2], xi[0] - xi[2]),
                    (xr[0] - xi[2], xi[0] + xr[2]),
                ]
                o = [
                    (xr[1] + xr[3], xi[1] + xi[3]),
                    (xr[1] + xi[3], xi[1] - xr[3]),
                    (xr[1] - xr[3], xi[1] - xi[3]),
                    (xr[1] - xi[3], xi[1] + xr[3]),
                ]
                t = [
                    o[0],
                    (root * (o[1][0] + o[1][1]), root * (o[1][1] - o[1][0])),
                    (o[2][1], -o[2][0]),
                    (root * (o[3][1] - o[3][0]), -root * (o[3][0] + o[3][1])),
                ]
                for k in range(4):
                    Y[k, top, cols] = (e[k][0] + t[k][0]).astype(bf16)
                    Y[k, low, cols] = (e[k][1] + t[k][1]).astype(bf16)
                    Y[k + 4, top, cols] = (e[k][0] - t[k][0]).astype(bf16)
                    Y[k + 4, low, cols] = (e[k][1] - t[k][1]).astype(bf16)
                return carry

            lax.fori_loop(0, 8, rows16, 0)
            return carry

        lax.fori_loop(0, 4, body, 0)

    scale = ANGLES ** (-0.5)

    def spectrum(half):
        def body(kk, carry):
            res = []
            ims = []
            for e in range(2):
                both = lax.dot_general(
                    tab[2 * kk + e], Y[2 * kk + e], NT, preferred_element_type=f32)
                res.append((both[:128, :128] + both[128:, 128:]) * scale)
                ims.append((both[:128, 128:] - both[128:, :128]) * scale)
            for t, parts in enumerate((res, ims)):
                val = jnp.concatenate([p.reshape(16, 8, 128) for p in parts], axis=1)
                val = val.reshape(8, 2, 16, 128)
                for c in range(2):
                    fst[half, c, :, kk, t] = val[:, c]
            return carry

        lax.fori_loop(0, 4, body, 0)

        def narrow(d, carry):
            psn[half, d] = fst[half, other, d].astype(bf16)
            return carry

        lax.fori_loop(0, 8, narrow, 0)

    def pair_copy(half):
        return pltpu.make_async_remote_copy(
            psn.at[half], prx.at[half], pair_s.at[half], pair_r.at[half],
            device_id={"pulse": buddy}, device_id_type=MESH)

    order = (4, 3, 5, 2, 6, 1, 7)

    def z_copy(half, k):
        return pltpu.make_async_remote_copy(
            zsn.at[half, (z + k) % 8], zrx.at[half, k - 1],
            z_s.at[half, k - 1], z_r.at[half, k - 1],
            device_id={"pulse": z_peer(k)}, device_id_type=MESH)

    def scatter(half):
        pair_copy(half).wait()

        def add(d, carry):
            zsn[half, d] = (fst[half, core, d] + prx[half, d].astype(f32)).astype(bf16)
            return carry

        lax.fori_loop(0, 8, add, 0)
        for k in order:
            z_copy(half, k).start()

    level1(0)
    level2(0)
    spectrum(0)
    pair_copy(0).start()
    level1(1)
    scatter(0)
    level2(1)
    spectrum(1)
    pair_copy(1).start()
    scatter(1)

    for half in range(2):
        total = fst[half, core, z] + prx[half, z].astype(f32)
        for k in order:
            z_copy(half, k).wait()
            total = total + zrx[half, k - 1].astype(f32)
        for kk in range(4):
            for t in range(2):
                G[64 * t + 16 * kk:64 * t + 16 * kk + 16, 128 * half:128 * half + 128] = total[kk, t]

    gg = G[...]
    m = lax.dot_general(gg, gg, NT, precision=lax.Precision.HIGHEST, preferred_element_type=f32)
    lane = lax.broadcasted_iota(jnp.int32, (64, 128), 1)
    sign = jnp.where(lane < 64, 1.0, -1.0).astype(f32)
    cov = m[:64] * sign + pltpu.roll(m[64:], 64, 1)

    def reduced(mine, here, buf, send, recv, axis_peer):
        buf[here] = mine
        copies = []
        for k in (2, 1, 3):
            copy = pltpu.make_async_remote_copy(
                buf.at[here], buf.at[here], send.at[k - 1], recv.at[k - 1],
                device_id={"range": axis_peer(k)}, device_id_type=MESH)
            copy.start()
            copies.append(copy)
        for copy in copies:
            copy.wait()
        return (buf[0] + buf[1]) + (buf[2] + buf[3])

    cov = reduced(cov, gx, cx, x_s, x_r, x_peer)
    cov = reduced(cov, gy, cy, y_s, y_r, y_peer)

    K = jnp.concatenate([cov * sign, pltpu.roll(cov, 64, 1)], axis=0)
    wide = lax.broadcasted_iota(jnp.int32, (128, 128), 1)
    w = jnp.sum(jnp.where(wide < 64, K, 0.0), axis=1, keepdims=True)
    v = w / jnp.sqrt(jnp.sum(w * w, axis=0, keepdims=True) + EPSILON)
    w = jnp.sum(K * v, axis=0, keepdims=True)
    v = w / jnp.sqrt(jnp.sum(w * w, axis=1, keepdims=True) + EPSILON)
    w = jnp.sum(K * v, axis=1, keepdims=True)
    v = w / jnp.sqrt(jnp.sum(w * w, axis=0, keepdims=True) + EPSILON)
    v = v * math.sqrt(BLOCK)
    vr = v[:64]
    vi = v[64:]
    gr = gg[:64]
    gi = gg[64:]
    focused = (gr * vr + gi * vi, gi * vr - gr * vi)
    for t in range(2):
        for k in range(8):
            for half in range(2):
                F[t, half, pl.ds(k, 8, stride=8), :] = focused[t][8 * k:8 * k + 8, 128 * half:128 * half + 128]
        for half in range(2):
            out[t, :, 128 * half:128 * half + 128] = F[t, half]


def per_device(pulse_data, merge_taps, merge_weights, squint):
    vmem = pl.BlockSpec(memory_space=pltpu.VMEM)
    dma = pltpu.SemaphoreType.DMA
    return pl.pallas_call(
        kernel,
        out_shape=jax.ShapeDtypeStruct((2, BLOCK, COLS), f32),
        in_specs=[vmem] * 4,
        out_specs=vmem,
        scratch_shapes=[
            pltpu.VMEM((2, 512, BEAMS), bf16),
            pltpu.VMEM((8, 16, BEAMS), f32),
            pltpu.VMEM((2, 16, BEAMS), f32),
            pltpu.VMEM((8, 4, BEAMS, 256), bf16),
            pltpu.VMEM((256, 256), bf16),
            pltpu.VMEM((8, 2, 2, 8, BEAMS), f32),
            pltpu.VMEM((8, 2, 8, BEAMS), f32),
            pltpu.VMEM((2, 256, BEAMS), bf16),
            pltpu.VMEM((2, 256, BEAMS), bf16),
            pltpu.VMEM((4, 256, 256), f32),
            pltpu.VMEM((8, 256, BEAMS), bf16),
            pltpu.VMEM((2, 16, BEAMS), f32),
            pltpu.VMEM((8, 256, BEAMS), bf16),
            pltpu.VMEM((2, 2, 8, 4, 2, 16, 128), f32),
            pltpu.VMEM((2, 8, 4, 2, 16, 128), bf16),
            pltpu.VMEM((2, 8, 4, 2, 16, 128), bf16),
            pltpu.VMEM((2, 8, 4, 2, 16, 128), bf16),
            pltpu.VMEM((2, 7, 4, 2, 16, 128), bf16),
            pltpu.VMEM((128, COLS), f32),
            pltpu.VMEM((2, 2, 64, 128), f32),
            pltpu.VMEM((4, 64, 128), f32),
            pltpu.VMEM((4, 64, 128), f32),
            dma, dma,
            dma((4,)), dma((4,)),
            dma((2,)), dma((2,)),
            dma((2, 7)), dma((2, 7)),
            dma((3,)), dma((3,)),
            dma((3,)), dma((3,)),
        ],
        compiler_params=pltpu.CompilerParams(
            collective_id=0, has_side_effects=True, vmem_limit_bytes=60 * 1024 * 1024),
    )(pulse_data, merge_taps, merge_weights, squint)


def solution(mesh):
    placed = (
        P(None, "pulse", "range"),
        P(None, None, None, "pulse"),
        P(None, None, None, "pulse"),
        P(None, "pulse"),
    )
    return jax.shard_map(
        per_device, mesh=mesh, in_specs=placed, out_specs=P(None, "pulse", "range"), check_vma=False
    )
```

profile of v0, /device:TPU:1, one launch (start us, length us, event | category | flops | bytes accessed | tf_op | source)
XLA Modules:
  0.0 61.6 jit_solution(2435386047646932821)
XLA Ops:
  0.0 60.1 %shard_map.46 = f32[2,64,256]{2,1,0:T(8,128)} custom-call(bf16[2,1024,256]{2,1,0:T(8,128)(2,1)} %data.1, s32[3,2,4,1024]{3,2,1,0:T(4,128)} %taps.1, bf16[3,2,4,1024]{3,2,1,0:T(4,128)(2,1)} %weights.1, f32[3,1024]{1,0:T(4,128)} %squint.1), custom_call_target="tpu_custom_call" | custom-call | tf_op jit(solution)/shard_map/pallas_call | solution.py:382
  60.1 1.6 %copy.6 = f32[2,64,256]{2,1,0:T(8,128)} copy(f32[2,64,256]{2,1,0:T(8,128)} %shard_map.46) | data formatting | bytes 262144
where the time goes:
time: 61.9 us; the launch traced here: 61.6 us
  Pallas kernels  60.1 us (97%)
  local copies, waits for them, and re-layouts  1.57 us (3%)
    pallas_call x1, Pallas kernels, per_device(): pl.pallas_call(kernel, out_shape=jax.ShapeDtypeStruct((2, BLOCK, COLS), f...  60.1 us
    unnamed x1, local copies, waits for them, and re-layouts  1.57 us

commit v1 on v0

v1 whole, which is shorter than its diff:
```python
import math

import jax
import jax.numpy as jnp
from jax import lax
from jax.experimental import pallas as pl
from jax.experimental.pallas import tpu as pltpu
from jax.sharding import PartitionSpec as P

RANGES = 4096
ANGLES = 16384
BEAMS = 1024
COLS = 256
BLOCK = 64
EPSILON = 1e-06
TWO_PI = 2.0 * math.pi
COS_TERMS = [(-1) ** k * TWO_PI ** (2 * k) / math.factorial(2 * k) for k in range(10)]
SIN_TERMS = [(-1) ** k * TWO_PI ** (2 * k + 1) / math.factorial(2 * k + 1) for k in range(9)]
MESH = pl.DeviceIdType.MESH
f32 = jnp.float32
bf16 = jnp.bfloat16
NT = (((1,), (1,)), ((), ()))


def flipped(index, bit):
    return index + bit - 2 * bit * ((index // bit) % 2)


def sincos(turns):
    part = turns - jnp.floor(turns + 0.5)
    y = part * part
    c = jnp.full_like(y, COS_TERMS[-1])
    for term in COS_TERMS[-2::-1]:
        c = c * y + term
    s = jnp.full_like(y, SIN_TERMS[-1])
    for term in SIN_TERMS[-2::-1]:
        s = s * y + term
    return c, s * part


def kernel(
    data_hbm, taps, weights, squint, out,
    data, dT, prm, snd, W, rowid, rb, rs, acc, S1, U, X, Y, us, tab,
    fst, stg, prx, zsn, zrx, G, F, cx,
    load_s, part_s, part_r, prm_s, prm_r, pair_s, pair_r, z_s, z_r, c_s, c_r,
):
    pulse = lax.axis_index("pulse")
    ranged = lax.axis_index("range")
    z = pulse // 2
    core = pulse % 2
    gx = ranged // 4
    gy = ranged % 4
    other = 1 - core
    buddy = flipped(pulse, 1)
    q2 = flipped(pulse, 2)
    q4 = flipped(pulse, 4)
    q6 = flipped(q2, 4)

    def z_peer(k):
        return ((z + k) % 8) * 2 + core

    def r_peer(k):
        return ((gx + k // 4) % 4) * 4 + (gy + k % 4) % 4

    load = pltpu.make_async_copy(data_hbm, data, load_s)
    load.start()

    barrier = pltpu.get_barrier_semaphore()
    pl.semaphore_signal(barrier, inc=1, device_id={"pulse": buddy}, device_id_type=MESH)
    for k in range(1, 8):
        pl.semaphore_signal(barrier, inc=1, device_id={"pulse": z_peer(k)}, device_id_type=MESH)
    for k in range(1, 16):
        pl.semaphore_signal(barrier, inc=1, device_id={"range": r_peer(k)}, device_id_type=MESH)

    def fill(ref, level, source):
        ref[0:4, :] = taps[level, source].astype(f32)
        ref[4:8, :] = weights[level, source].astype(f32)
        ref[8:9, :] = squint[level:level + 1, :]

    fill(snd.at[0], 1, 1)
    fill(snd.at[1], 2, 1)
    fill(prm.at[4], 2, 0)
    fill(prm.at[0], 0, 0)
    fill(prm.at[1], 0, 1)
    fill(prm.at[2], 1, 0)
    rowid[...] = lax.broadcasted_iota(jnp.int32, (256, 256), 0).astype(f32).astype(bf16)

    def build(m, slot):
        for nt in range(4):
            cols = slice(256 * nt, 256 * nt + 256)
            places = [prm[m, tap:tap + 1, cols] for tap in range(4)]
            scales = [prm[m, 4 + tap:5 + tap, cols].astype(bf16) for tap in range(4)]
            for kb in range(4):
                val = jnp.zeros((256, 256), bf16)
                for tap in range(4):
                    here = rowid[...] == (places[tap] - 256.0 * kb).astype(bf16)
                    val = jnp.where(here, scales[tap], val)
                W[slot, 256 * kb:256 * kb + 256, cols] = val

    first_range = (ranged * COLS).astype(f32)

    def prepare_rotation(m):
        slope = prm[m, 8:9, :]
        i8 = lax.broadcasted_iota(jnp.int32, (8, BEAMS), 0).astype(f32)
        c0, s0 = sincos(slope * ((i8 + first_range) * (1.0 / RANGES)))
        cf, sf = sincos(slope * (jnp.where(i8 < 1.0, 8.0, 128.0) * (1.0 / RANGES)))
        rb[m, 0, 0] = c0
        rb[m, 0, 1] = s0
        ch = cf[1:2]
        sh = sf[1:2]
        rb[m, 1, 0] = c0 * ch - s0 * sh
        rb[m, 1, 1] = s0 * ch + c0 * sh
        rs[m, 0] = jnp.broadcast_to(cf[0:1], (8, BEAMS))
        rs[m, 1] = jnp.broadcast_to(sf[0:1], (8, BEAMS))

    def rotate(src, m, half, dest, kind, re_at, im_at):
        for nt in range(4):
            cols = slice(256 * nt, 256 * nt + 256)
            c = rb[m, half, 0, :, cols]
            s = rb[m, half, 1, :, cols]
            c8 = rs[m, 0, :, cols]
            s8 = rs[m, 1, :, cols]
            for i in range(8):
                reals = []
                imags = []
                for e in range(2):
                    q = 16 * i + 8 * e
                    a = src[re_at + q:re_at + q + 8, cols]
                    b = src[im_at + q:im_at + q + 8, cols]
                    reals.append(c * a - s * b)
                    imags.append(s * a + c * b)
                    c, s = c * c8 - s * s8, s * c8 + c * s8
                q = 128 * half + 16 * i
                dest[q:q + 16, cols] = jnp.concatenate(reals, axis=0).astype(kind)
                dest[256 + q:272 + q, cols] = jnp.concatenate(imags, axis=0).astype(kind)

    def rotate_all(src, m, dest, kind):
        for half in range(2):
            rotate(src, m, half, dest, kind, 128 * half, 256 + 128 * half)

    first_angle = BEAMS * (core + 8 * (z // 4))

    def table_base():
        angle = lax.broadcasted_iota(jnp.int32, (16, BEAMS), 1) + first_angle
        up = lax.broadcasted_iota(jnp.int32, (16, BEAMS), 0)
        us[0], us[1] = sincos(((64 * up * angle) % ANGLES).astype(f32) * (1.0 / ANGLES))

    def table(k):
        a8 = lax.broadcasted_iota(jnp.int32, (8, BEAMS), 1) + first_angle
        v8 = 8 * lax.broadcasted_iota(jnp.int32, (8, BEAMS), 0) + k
        vc, vs = sincos(((v8 * a8) % ANGLES).astype(f32) * (1.0 / ANGLES))
        for pair in range(8):
            cs = []
            ss = []
            for u in (2 * pair, 2 * pair + 1):
                uc = us[0, u:u + 1, :]
                un = us[1, u:u + 1, :]
                cs.append(uc * vc - un * vs)
                ss.append(un * vc + uc * vs)
            tab[k, 16 * pair:16 * pair + 16, :] = jnp.concatenate(cs, axis=0).astype(bf16)
            tab[k, 128 + 16 * pair:144 + 16 * pair, :] = jnp.concatenate(ss, axis=0).astype(bf16)

    build(0, 0)
    prepare_rotation(0)
    table_base()

    load.wait()
    for t in range(2):
        dT[0, t * COLS:(t + 1) * COLS, :] = data[t].T

    pl.semaphore_wait(barrier, 23)

    part = pltpu.make_async_remote_copy(
        dT.at[0], dT.at[1], part_s, part_r, device_id={"pulse": buddy}, device_id_type=MESH)
    part.start()
    prm_copies = []
    for n, (src, slot, target) in enumerate((
        (snd.at[1], 7, q6), (snd.at[1], 5, q4), (snd.at[0], 3, q2), (prm.at[4], 6, q2))):
        copy = pltpu.make_async_remote_copy(
            src, prm.at[slot], prm_s.at[n], prm_r.at[n],
            device_id={"pulse": target}, device_id_type=MESH)
        copy.start()
        prm_copies.append(copy)

    acc[0] = jnp.dot(dT[0], W[0], preferred_element_type=f32)
    build(1, 1)
    prepare_rotation(2)
    table(0)
    part.wait()
    acc[1] = jnp.dot(dT[1], W[1], preferred_element_type=f32) + acc[0]
    build(2, 0)
    table(1)
    for copy in prm_copies:
        copy.wait()
    rotate_all(acc.at[1], 0, S1, bf16)

    acc[0] = jnp.dot(S1[...], W[0], preferred_element_type=f32)
    build(3, 1)
    prepare_rotation(3)
    table(2)

    acc[1] = jnp.dot(S1[...], W[1], preferred_element_type=f32)
    build(4, 0)
    rotate_all(acc.at[0], 2, U.at[0], bf16)
    prepare_rotation(4)
    table(3)

    bit0 = z % 2
    bit1 = (z // 2) % 2

    def slot_of(i):
        at0 = bit0 if i % 2 == 0 else 1 - bit0
        at1 = bit1 if i // 2 == 0 else 1 - bit1
        return at0 + 2 * at1

    acc[0] = jnp.dot(U[0], W[0], preferred_element_type=f32)
    build(5, 1)
    rotate_all(acc.at[1], 3, U.at[1], bf16)
    prepare_rotation(5)
    table(4)

    acc[1] = jnp.dot(U[0], W[1], preferred_element_type=f32)
    build(6, 0)
    rotate_all(acc.at[0], 4, X.at[slot_of(0)], f32)
    prepare_rotation(6)
    table(5)

    acc[0] = jnp.dot(U[1], W[0], preferred_element_type=f32)
    build(7, 1)
    rotate_all(acc.at[1], 5, X.at[slot_of(2)], f32)
    prepare_rotation(7)
    table(6)

    def last(half):
        lhs = jnp.concatenate(
            [U[1, 128 * half:128 * half + 128, :], U[1, 256 + 128 * half:384 + 128 * half, :]], axis=0)
        acc[1, 256 * half:256 * half + 256, :] = jnp.dot(lhs, W[1], preferred_element_type=f32)

    root = math.sqrt(0.5)

    def combine(half, nt):
        cols = pl.ds(nt * 256, 256) if isinstance(nt, int) else pl.ds(pl.multiple_of(nt * 256, 256), 256)
        for step in range(8):
            top = slice(128 * half + 16 * step, 128 * half + 16 * step + 16)
            low = slice(256 + 128 * half + 16 * step, 272 + 128 * half + 16 * step)
            xr = [X[n, top, cols] for n in range(4)]
            xi = [X[n, low, cols] for n in range(4)]
            e = [
                (xr[0] + xr[2], xi[0] + xi[2]),
                (xr[0] + xi[2], xi[0] - xr[2]),
                (xr[0] - xr[2], xi[0] - xi[2]),
                (xr[0] - xi[2], xi[0] + xr[2]),
            ]
            o = [
                (xr[1] + xr[3], xi[1] + xi[3]),
                (xr[1] + xi[3], xi[1] - xr[3]),
                (xr[1] - xr[3], xi[1] - xi[3]),
                (xr[1] - xi[3], xi[1] + xr[3]),
            ]
            t = [
                o[0],
                (root * (o[1][0] + o[1][1]), root * (o[1][1] - o[1][0])),
                (o[2][1], -o[2][0]),
                (root * (o[3][1] - o[3][0]), -root * (o[3][0] + o[3][1])),
            ]
            top = slice(16 * step, 16 * step + 16)
            low = slice(128 + 16 * step, 144 + 16 * step)
            for k in range(4):
                Y[half, k, top, cols] = (e[k][0] + t[k][0]).astype(bf16)
                Y[half, k, low, cols] = (e[k][1] + t[k][1]).astype(bf16)
                Y[half, k + 4, top, cols] = (e[k][0] - t[k][0]).astype(bf16)
                Y[half, k + 4, low, cols] = (e[k][1] - t[k][1]).astype(bf16)

    scale = ANGLES ** (-0.5)

    def spectrum(half, beside):
        def body(kk, carry):
            res = []
            ims = []
            for e in range(2):
                both = lax.dot_general(
                    tab[2 * kk + e], Y[half, 2 * kk + e], NT, preferred_element_type=f32)
                res.append((both[:128, :128] + both[128:, 128:]) * scale)
                ims.append((both[:128, 128:] - both[128:, :128]) * scale)
            for t, parts in enumerate((res, ims)):
                val = jnp.concatenate([p.reshape(16, 8, 128) for p in parts], axis=1)
                val = val.reshape(8, 2, 16, 128)
                for c in range(2):
                    fst[half, c, :, kk, t] = val[:, c]
                    stg[half, c, :, kk, t] = val[:, c].astype(bf16)
            if beside is not None:
                combine(beside, kk)
            return carry

        lax.fori_loop(0, 4, body, 0)

    def pair_copy(half):
        return pltpu.make_async_remote_copy(
            stg.at[half, other], prx.at[half], pair_s.at[half], pair_r.at[half],
            device_id={"pulse": buddy}, device_id_type=MESH)

    order = (4, 3, 5, 2, 6, 1, 7)

    def z_copy(half, k):
        return pltpu.make_async_remote_copy(
            zsn.at[half, (z + k) % 8], zrx.at[half, k - 1],
            z_s.at[half, k - 1], z_r.at[half, k - 1],
            device_id={"pulse": z_peer(k)}, device_id_type=MESH)

    def scatter(half):
        pair_copy(half).wait()
        for d in range(8):
            zsn[half, d] = (fst[half, core, d] + prx[half, d].astype(f32)).astype(bf16)
        for k in order:
            z_copy(half, k).start()

    last(0)
    rotate_all(acc.at[0], 6, X.at[slot_of(1)], f32)
    table(7)
    rotate(acc.at[1], 7, 0, X.at[slot_of(3)], f32, 0, 128)
    last(1)
    for nt in range(4):
        combine(0, nt)
    rotate(acc.at[1], 7, 1, X.at[slot_of(3)], f32, 256, 384)
    spectrum(0, 1)
    pair_copy(0).start()
    scatter(0)
    spectrum(1, None)
    pair_copy(1).start()
    scatter(1)

    for half in range(2):
        total = fst[half, core, z] + prx[half, z].astype(f32)
        for k in order:
            z_copy(half, k).wait()
            total = total + zrx[half, k - 1].astype(f32)
        for kk in range(4):
            for t in range(2):
                G[64 * t + 16 * kk:64 * t + 16 * kk + 16, 128 * half:128 * half + 128] = total[kk, t]

    gg = G[...]
    m = lax.dot_general(gg, gg, NT, precision=lax.Precision.HIGHEST, preferred_element_type=f32)
    lane = lax.broadcasted_iota(jnp.int32, (64, 128), 1)
    row = lax.broadcasted_iota(jnp.int32, (64, 128), 0)
    sign = jnp.where(lane < 64, 1.0, -1.0).astype(f32)
    cov = m[:64] * sign + pltpu.roll(m[64:], 64, 1)
    packed = jnp.where(lane <= row, cov, pltpu.roll(cov, 64, 1))
    packed = jnp.where(lane[:32] < 64, packed[:32], pltpu.roll(packed[32:], 64, 1))

    cx[ranged] = packed
    copies = []
    for k in (10, 9, 11, 6, 14, 2, 8, 5, 7, 13, 15, 1, 3, 4, 12):
        copy = pltpu.make_async_remote_copy(
            cx.at[ranged], cx.at[ranged], c_s.at[k - 1], c_r.at[k - 1],
            device_id={"range": r_peer(k)}, device_id_type=MESH)
        copy.start()
        copies.append(copy)
    for copy in copies:
        copy.wait()
    sums = [cx[n] for n in range(16)]
    while len(sums) > 1:
        sums = [sums[n] + sums[n + 1] for n in range(0, len(sums), 2)]
    packed = jnp.concatenate([sums[0], pltpu.roll(sums[0], 64, 1)], axis=0)
    square = jnp.concatenate([packed, packed], axis=0)
    flip = square.T[:64]
    c_re = jnp.where(lane <= row, packed, flip)
    c_im = jnp.where(lane > row, packed, jnp.where(lane < row, -flip, 0.0))

    K = jnp.concatenate([
        jnp.where(lane < 64, c_re, -pltpu.roll(c_im, 64, 1)),
        jnp.where(lane < 64, c_im, pltpu.roll(c_re, 64, 1)),
    ], axis=0)
    wide = lax.broadcasted_iota(jnp.int32, (128, 128), 1)
    w = jnp.sum(jnp.where(wide < 64, K, 0.0), axis=1, keepdims=True)
    v = w / jnp.sqrt(jnp.sum(w * w, axis=0, keepdims=True) + EPSILON)
    w = jnp.sum(K * v, axis=0, keepdims=True)
    v = w / jnp.sqrt(jnp.sum(w * w, axis=1, keepdims=True) + EPSILON)
    w = jnp.sum(K * v, axis=1, keepdims=True)
    v = w / jnp.sqrt(jnp.sum(w * w, axis=0, keepdims=True) + EPSILON)
    v = v * math.sqrt(BLOCK)
    vr = v[:64]
    vi = v[64:]
    gr = gg[:64]
    gi = gg[64:]
    focused = (gr * vr + gi * vi, gi * vr - gr * vi)
    for t in range(2):
        for k in range(8):
            for half in range(2):
                F[t, half, pl.ds(k, 8, stride=8), :] = focused[t][8 * k:8 * k + 8, 128 * half:128 * half + 128]
        for half in range(2):
            out[t, :, 128 * half:128 * half + 128] = F[t, half]


def per_device(pulse_data, merge_taps, merge_weights, squint):
    vmem = pl.BlockSpec(memory_space=pltpu.VMEM)
    dma = pltpu.SemaphoreType.DMA
    return pl.pallas_call(
        kernel,
        out_shape=jax.ShapeDtypeStruct((2, BLOCK, COLS), f32),
        in_specs=[pl.BlockSpec(memory_space=pl.ANY)] + [vmem] * 3,
        out_specs=vmem,
        scratch_shapes=[
            pltpu.VMEM((2, BEAMS, COLS), bf16),
            pltpu.VMEM((2, 512, BEAMS), bf16),
            pltpu.VMEM((8, 16, BEAMS), f32),
            pltpu.VMEM((2, 16, BEAMS), f32),
            pltpu.VMEM((2, BEAMS, BEAMS), bf16),
            pltpu.VMEM((256, 256), bf16),
            pltpu.VMEM((8, 2, 2, 8, BEAMS), f32),
            pltpu.VMEM((8, 2, 8, BEAMS), f32),
            pltpu.VMEM((2, 512, BEAMS), f32),
            pltpu.VMEM((512, BEAMS), bf16),
            pltpu.VMEM((2, 512, BEAMS), bf16),
            pltpu.VMEM((4, 512, BEAMS), f32),
            pltpu.VMEM((2, 8, 256, BEAMS), bf16),
            pltpu.VMEM((2, 16, BEAMS), f32),
            pltpu.VMEM((8, 256, BEAMS), bf16),
            pltpu.VMEM((2, 2, 8, 4, 2, 16, 128), f32),
            pltpu.VMEM((2, 2, 8, 4, 2, 16, 128), bf16),
            pltpu.VMEM((2, 8, 4, 2, 16, 128), bf16),
            pltpu.VMEM((2, 8, 4, 2, 16, 128), bf16),
            pltpu.VMEM((2, 7, 4, 2, 16, 128), bf16),
            pltpu.VMEM((128, COLS), f32),
            pltpu.VMEM((2, 2, 64, 128), f32),
            pltpu.VMEM((16, 32, 128), f32),
            dma, dma, dma,
            dma((4,)), dma((4,)),
            dma((2,)), dma((2,)),
            dma((2, 7)), dma((2, 7)),
            dma((15,)), dma((15,)),
        ],
        compiler_params=pltpu.CompilerParams(
            collective_id=0, has_side_effects=True, vmem_limit_bytes=60 * 1024 * 1024),
    )(pulse_data, merge_taps, merge_weights, squint)


def solution(mesh):
    placed = (
        P(None, "pulse", "range"),
        P(None, None, None, "pulse"),
        P(None, None, None, "pulse"),
        P(None, "pulse"),
    )
    return jax.shard_map(
        per_device, mesh=mesh, in_specs=placed, out_specs=P(None, "pulse", "range"), check_vma=False
    )
```

time: 61.9 us -> 58.4 us (0.943)
  Pallas kernels: 60.1 us -> 56.7 us
    pallas_call x1, Pallas kernels: 60.1 us -> 56.7 us  [per_device(): pl.pallas_call(kernel, out_shape=jax.ShapeDtypeStruct((2, BLOCK, COLS), f...]
where the time goes in v1:
time: 58.4 us; the launch traced here: 58.3 us
  Pallas kernels  56.7 us (97%)
  local copies, waits for them, and re-layouts  1.57 us (3%)
    pallas_call x1, Pallas kernels, per_device(): pl.pallas_call(kernel, out_shape=jax.ShapeDtypeStruct((2, BLOCK, COLS), f...  56.7 us
    unnamed x1, local copies, waits for them, and re-layouts  1.57 us

profile of v1, /device:TPU:1, one launch (start us, length us, event | category | flops | bytes accessed | tf_op | source)
XLA Modules:
  0.0 58.3 jit_solution(7193228021888429067)
XLA Ops:
  0.0 56.7 %shard_map.46 = f32[2,64,256]{2,1,0:T(8,128)} custom-call(bf16[2,1024,256]{2,1,0:T(8,128)(2,1)} %data_hbm.1, s32[3,2,4,1024]{3,2,1,0:T(4,128)} %taps.1, bf16[3,2,4,1024]{3,2,1,0:T(4,128)(2,1)} %weights.1, f32[3,1024]{1,0:T(4,128)} %squint.1), custom_call_target="tpu_custom_call" | custom-call | tf_op jit(solution)/shard_map/pallas_call | solution.py:397
  56.7 1.6 %copy.6 = f32[2,64,256]{2,1,0:T(8,128)} copy(f32[2,64,256]{2,1,0:T(8,128)} %shard_map.46) | data formatting | bytes 262144

commit v2 on v1

--- a/solution.py
+++ b/solution.py
@@ -41,8 +41,9 @@
 def kernel(
     data_hbm, taps, weights, squint, out,
     data, dT, prm, snd, W, rowid, rb, rs, acc, S1, U, X, Y, us, tab,
-    fst, stg, prx, zsn, zrx, G, F, cx,
-    load_s, part_s, part_r, prm_s, prm_r, pair_s, pair_r, z_s, z_r, c_s, c_r,
+    fst, stg, prx, zsn, near, far, cmb, zrx, G, F, cx,
+    load_s, part_s, part_r, prm_s, prm_r, pair_s, pair_r,
+    near_s, near_r, far_s, far_r, z_s, z_r, c_s, c_r,
 ):
     pulse = lax.axis_index("pulse")
     ranged = lax.axis_index("range")
@@ -67,15 +68,21 @@
 
     barrier = pltpu.get_barrier_semaphore()
     pl.semaphore_signal(barrier, inc=1, device_id={"pulse": buddy}, device_id_type=MESH)
-    for k in range(1, 8):
+    pl.semaphore_signal(barrier, inc=1, device_id={"pulse": q6}, device_id_type=MESH)
+    for k in (1, 2, 6, 7):
         pl.semaphore_signal(barrier, inc=1, device_id={"pulse": z_peer(k)}, device_id_type=MESH)
     for k in range(1, 16):
         pl.semaphore_signal(barrier, inc=1, device_id={"range": r_peer(k)}, device_id_type=MESH)
 
     def fill(ref, level, source):
-        ref[0:4, :] = taps[level, source].astype(f32)
-        ref[4:8, :] = weights[level, source].astype(f32)
-        ref[8:9, :] = squint[level:level + 1, :]
+        tap = taps[level, source]
+        slope = squint[level:level + 1, :]
+        first = slope.astype(bf16).astype(f32)
+        second = (slope - first).astype(bf16).astype(f32)
+        third = slope - first - second
+        ref[...] = jnp.concatenate([
+            (tap % 256).astype(f32), (tap // 256).astype(f32), weights[level, source].astype(f32),
+            first, second, third, jnp.zeros_like(slope)], axis=0).astype(bf16)
 
     fill(snd.at[0], 1, 1)
     fill(snd.at[1], 2, 1)
@@ -88,8 +95,9 @@
     def build(m, slot):
         for nt in range(4):
             cols = slice(256 * nt, 256 * nt + 256)
-            places = [prm[m, tap:tap + 1, cols] for tap in range(4)]
-            scales = [prm[m, 4 + tap:5 + tap, cols].astype(bf16) for tap in range(4)]
+            rows = prm[m, :, cols].astype(f32)
+            places = [rows[tap:tap + 1] + 256.0 * rows[4 + tap:5 + tap] for tap in range(4)]
+            scales = [rows[8 + tap:9 + tap].astype(bf16) for tap in range(4)]
             for kb in range(4):
                 val = jnp.zeros((256, 256), bf16)
                 for tap in range(4):
@@ -100,7 +108,8 @@
     first_range = (ranged * COLS).astype(f32)
 
     def prepare_rotation(m):
-        slope = prm[m, 8:9, :]
+        rows = prm[m].astype(f32)
+        slope = rows[12:13] + rows[13:14] + rows[14:15]
         i8 = lax.broadcasted_iota(jnp.int32, (8, BEAMS), 0).astype(f32)
         c0, s0 = sincos(slope * ((i8 + first_range) * (1.0 / RANGES)))
         cf, sf = sincos(slope * (jnp.where(i8 < 1.0, 8.0, 128.0) * (1.0 / RANGES)))
@@ -168,14 +177,14 @@
     for t in range(2):
         dT[0, t * COLS:(t + 1) * COLS, :] = data[t].T
 
-    pl.semaphore_wait(barrier, 23)
+    pl.semaphore_wait(barrier, 21)
 
     part = pltpu.make_async_remote_copy(
         dT.at[0], dT.at[1], part_s, part_r, device_id={"pulse": buddy}, device_id_type=MESH)
     part.start()
     prm_copies = []
     for n, (src, slot, target) in enumerate((
-        (snd.at[1], 7, q6), (snd.at[1], 5, q4), (snd.at[0], 3, q2), (prm.at[4], 6, q2))):
+        (snd.at[0], 3, q2), (snd.at[1], 5, q4), (prm.at[4], 6, q2), (snd.at[1], 7, q6))):
         copy = pltpu.make_async_remote_copy(
             src, prm.at[slot], prm_s.at[n], prm_r.at[n],
             device_id={"pulse": target}, device_id_type=MESH)
@@ -190,11 +199,10 @@
     acc[1] = jnp.dot(dT[1], W[1], preferred_element_type=f32) + acc[0]
     build(2, 0)
     table(1)
-    for copy in prm_copies:
-        copy.wait()
     rotate_all(acc.at[1], 0, S1, bf16)
 
     acc[0] = jnp.dot(S1[...], W[0], preferred_element_type=f32)
+    prm_copies[0].wait()
     build(3, 1)
     prepare_rotation(3)
     table(2)
@@ -214,18 +222,21 @@
         return at0 + 2 * at1
 
     acc[0] = jnp.dot(U[0], W[0], preferred_element_type=f32)
+    prm_copies[1].wait()
     build(5, 1)
     rotate_all(acc.at[1], 3, U.at[1], bf16)
     prepare_rotation(5)
     table(4)
 
     acc[1] = jnp.dot(U[0], W[1], preferred_element_type=f32)
+    prm_copies[2].wait()
     build(6, 0)
     rotate_all(acc.at[0], 4, X.at[slot_of(0)], f32)
     prepare_rotation(6)
     table(5)
 
     acc[0] = jnp.dot(U[1], W[0], preferred_element_type=f32)
+    prm_copies[3].wait()
     build(7, 1)
     rotate_all(acc.at[1], 5, X.at[slot_of(2)], f32)
     prepare_rotation(7)
@@ -239,7 +250,7 @@
     root = math.sqrt(0.5)
 
     def combine(half, nt):
-        cols = pl.ds(nt * 256, 256) if isinstance(nt, int) else pl.ds(pl.multiple_of(nt * 256, 256), 256)
+        cols = slice(256 * nt, 256 * nt + 256)
         for step in range(8):
             top = slice(128 * half + 16 * step, 128 * half + 16 * step + 16)
             low = slice(256 + 128 * half + 16 * step, 272 + 128 * half + 16 * step)
@@ -273,46 +284,72 @@
 
     scale = ANGLES ** (-0.5)
 
-    def spectrum(half, beside):
-        def body(kk, carry):
+    def spectrum(piece, beside):
+        half = piece // 2
+        for j in range(2):
+            kk = 2 * (piece % 2) + j
             res = []
             ims = []
-            for e in range(2):
-                both = lax.dot_general(
-                    tab[2 * kk + e], Y[half, 2 * kk + e], NT, preferred_element_type=f32)
+            for k in (2 * kk, 2 * kk + 1):
+                both = lax.dot_general(tab[k], Y[half, k], NT, preferred_element_type=f32)
                 res.append((both[:128, :128] + both[128:, 128:]) * scale)
                 ims.append((both[:128, 128:] - both[128:, :128]) * scale)
             for t, parts in enumerate((res, ims)):
                 val = jnp.concatenate([p.reshape(16, 8, 128) for p in parts], axis=1)
                 val = val.reshape(8, 2, 16, 128)
                 for c in range(2):
-                    fst[half, c, :, kk, t] = val[:, c]
-                    stg[half, c, :, kk, t] = val[:, c].astype(bf16)
+                    fst[piece, c, :, j, t] = val[:, c]
+                    stg[piece, c, :, j, t] = val[:, c].astype(bf16)
             if beside is not None:
                 combine(beside, kk)
-            return carry
-
-        lax.fori_loop(0, 4, body, 0)
-
-    def pair_copy(half):
+
+    def to(src, dst, send, recv, target):
         return pltpu.make_async_remote_copy(
-            stg.at[half, other], prx.at[half], pair_s.at[half], pair_r.at[half],
-            device_id={"pulse": buddy}, device_id_type=MESH)
-
-    order = (4, 3, 5, 2, 6, 1, 7)
-
-    def z_copy(half, k):
-        return pltpu.make_async_remote_copy(
-            zsn.at[half, (z + k) % 8], zrx.at[half, k - 1],
-            z_s.at[half, k - 1], z_r.at[half, k - 1],
-            device_id={"pulse": z_peer(k)}, device_id_type=MESH)
-
-    def scatter(half):
-        pair_copy(half).wait()
+            src, dst, send, recv, device_id={"pulse": target}, device_id_type=MESH)
+
+    def pair(piece):
+        return to(stg.at[piece, other], prx.at[piece], pair_s.at[piece], pair_r.at[piece], buddy)
+
+    def at(k):
+        return (z + k) % 8
+
+    def near_copy(piece, n):
+        return to(zsn.at[piece, at((3, 5)[n])], near.at[piece, n],
+                  near_s.at[piece, n], near_r.at[piece, n], z_peer((1, 7)[n]))
+
+    def far_copy(piece, n):
+        return to(zsn.at[piece, at(4), :, n], far.at[piece, n],
+                  far_s.at[piece, n], far_r.at[piece, n], z_peer((2, 6)[n]))
+
+    def z_copy(piece, n):
+        src = cmb.at[piece, n] if n < 2 else zsn.at[piece, at((1, 7)[n - 2])]
+        return to(src, zrx.at[piece, n], z_s.at[piece, n], z_r.at[piece, n], z_peer((2, 6, 1, 7)[n]))
+
+    def relay(piece):
+        pair(piece).wait()
         for d in range(8):
-            zsn[half, d] = (fst[half, core, d] + prx[half, d].astype(f32)).astype(bf16)
-        for k in order:
-            z_copy(half, k).start()
+            both = fst[piece, core, d] + prx[piece, d].astype(f32)
+            fst[piece, core, d] = both
+            zsn[piece, d] = both.astype(bf16)
+        for n in range(2):
+            far_copy(piece, n).start()
+        for n in range(2):
+            near_copy(piece, n).start()
+        for n in range(2, 4):
+            z_copy(piece, n).start()
+
+    def scatter(piece):
+        for n in range(2):
+            far_copy(piece, n).wait()
+            near_copy(piece, n).wait()
+            dest = at((2, 6)[n])
+            for j in range(2):
+                for t in range(2):
+                    both = fst[piece, core, dest, j, t] + near[piece, n, j, t].astype(f32)
+                    if t == n:
+                        both = both + far[piece, n, j].astype(f32)
+                    cmb[piece, n, j, t] = both.astype(bf16)
+            z_copy(piece, n).start()
 
     last(0)
     rotate_all(acc.at[0], 6, X.at[slot_of(1)], f32)
@@ -323,20 +360,32 @@
         combine(0, nt)
     rotate(acc.at[1], 7, 1, X.at[slot_of(3)], f32, 256, 384)
     spectrum(0, 1)
-    pair_copy(0).start()
+    pair(0).start()
+    spectrum(1, 1)
+    pair(1).start()
+    relay(0)
+    spectrum(2, None)
+    pair(2).start()
+    relay(1)
     scatter(0)
-    spectrum(1, None)
-    pair_copy(1).start()
+    spectrum(3, None)
+    pair(3).start()
+    relay(2)
     scatter(1)
-
-    for half in range(2):
-        total = fst[half, core, z] + prx[half, z].astype(f32)
-        for k in order:
-            z_copy(half, k).wait()
-            total = total + zrx[half, k - 1].astype(f32)
-        for kk in range(4):
+    relay(3)
+    scatter(2)
+    scatter(3)
+
+    for piece in range(4):
+        total = fst[piece, core, z]
+        for n in range(4):
+            z_copy(piece, n).wait()
+            total = total + zrx[piece, n].astype(f32)
+        for j in range(2):
+            kk = 2 * (piece % 2) + j
             for t in range(2):
-                G[64 * t + 16 * kk:64 * t + 16 * kk + 16, 128 * half:128 * half + 128] = total[kk, t]
+                here = 128 * (piece // 2)
+                G[64 * t + 16 * kk:64 * t + 16 * kk + 16, here:here + 128] = total[j, t]
 
     gg = G[...]
     m = lax.dot_general(gg, gg, NT, precision=lax.Precision.HIGHEST, preferred_element_type=f32)
@@ -402,8 +451,8 @@
         scratch_shapes=[
             pltpu.VMEM((2, BEAMS, COLS), bf16),
             pltpu.VMEM((2, 512, BEAMS), bf16),
-            pltpu.VMEM((8, 16, BEAMS), f32),
-            pltpu.VMEM((2, 16, BEAMS), f32),
+            pltpu.VMEM((8, 16, BEAMS), bf16),
+            pltpu.VMEM((2, 16, BEAMS), bf16),
             pltpu.VMEM((2, BEAMS, BEAMS), bf16),
             pltpu.VMEM((256, 256), bf16),
             pltpu.VMEM((8, 2, 2, 8, BEAMS), f32),
@@ -415,18 +464,23 @@
             pltpu.VMEM((2, 8, 256, BEAMS), bf16),
             pltpu.VMEM((2, 16, BEAMS), f32),
             pltpu.VMEM((8, 256, BEAMS), bf16),
-            pltpu.VMEM((2, 2, 8, 4, 2, 16, 128), f32),
-            pltpu.VMEM((2, 2, 8, 4, 2, 16, 128), bf16),
-            pltpu.VMEM((2, 8, 4, 2, 16, 128), bf16),
-            pltpu.VMEM((2, 8, 4, 2, 16, 128), bf16),
-            pltpu.VMEM((2, 7, 4, 2, 16, 128), bf16),
+            pltpu.VMEM((4, 2, 8, 2, 2, 16, 128), f32),
+            pltpu.VMEM((4, 2, 8, 2, 2, 16, 128), bf16),
+            pltpu.VMEM((4, 8, 2, 2, 16, 128), bf16),
+            pltpu.VMEM((4, 8, 2, 2, 16, 128), bf16),
+            pltpu.VMEM((4, 2, 2, 2, 16, 128), bf16),
+            pltpu.VMEM((4, 2, 2, 16, 128), bf16),
+            pltpu.VMEM((4, 2, 2, 2, 16, 128), bf16),
+            pltpu.VMEM((4, 4, 2, 2, 16, 128), bf16),
             pltpu.VMEM((128, COLS), f32),
             pltpu.VMEM((2, 2, 64, 128), f32),
             pltpu.VMEM((16, 32, 128), f32),
             dma, dma, dma,
             dma((4,)), dma((4,)),
-            dma((2,)), dma((2,)),
-            dma((2, 7)), dma((2, 7)),
+            dma((4,)), dma((4,)),
+            dma((4, 2)), dma((4, 2)),
+            dma((4, 2)), dma((4, 2)),
+            dma((4, 4)), dma((4, 4)),
             dma((15,)), dma((15,)),
         ],
         compiler_params=pltpu.CompilerParams(

time: 58.4 us -> 51.2 us (0.88)
  Pallas kernels: 56.7 us -> 49.1 us
    pallas_call x1, Pallas kernels: 56.7 us -> 49.1 us  [per_device(): pl.pallas_call(kernel, out_shape=jax.ShapeDtypeStruct((2, BLOCK, COLS), f...]
where the time goes in v2:
time: 51.2 us; the launch traced here: 50.6 us
  Pallas kernels  49.1 us (96%)
  local copies, waits for them, and re-layouts  1.57 us (3%)
    pallas_call x1, Pallas kernels, per_device(): pl.pallas_call(kernel, out_shape=jax.ShapeDtypeStruct((2, BLOCK, COLS), f...  49.1 us
    unnamed x1, local copies, waits for them, and re-layouts  1.57 us

profile of v2, /device:TPU:1, one launch (start us, length us, event | category | flops | bytes accessed | tf_op | source)
XLA Modules:
  0.0 50.6 jit_solution(3822914196976705182)
XLA Ops:
  0.0 49.1 %shard_map.46 = f32[2,64,256]{2,1,0:T(8,128)} custom-call(bf16[2,1024,256]{2,1,0:T(8,128)(2,1)} %data_hbm.1, s32[3,2,4,1024]{3,2,1,0:T(4,128)} %taps.1, bf16[3,2,4,1024]{3,2,1,0:T(4,128)(2,1)} %weights.1, f32[3,1024]{1,0:T(4,128)} %squint.1), custom_call_target="tpu_custom_call" | custom-call | tf_op jit(solution)/shard_map/pallas_call | solution.py:446
  49.1 1.6 %copy.6 = f32[2,64,256]{2,1,0:T(8,128)} copy(f32[2,64,256]{2,1,0:T(8,128)} %shard_map.46) | data formatting | bytes 262144

commit v3 on v1

--- a/solution.py
+++ b/solution.py
@@ -20,6 +20,7 @@
 f32 = jnp.float32
 bf16 = jnp.bfloat16
 NT = (((1,), (1,)), ((), ()))
+STEPS = (4, 3, 5, 0, 1, 2, 6, 7)
 
 
 def flipped(index, bit):
@@ -41,8 +42,9 @@
 def kernel(
     data_hbm, taps, weights, squint, out,
     data, dT, prm, snd, W, rowid, rb, rs, acc, S1, U, X, Y, us, tab,
-    fst, stg, prx, zsn, zrx, G, F, cx,
-    load_s, part_s, part_r, prm_s, prm_r, pair_s, pair_r, z_s, z_r, c_s, c_r,
+    fst, stg, prx, zsn, near, far, zrx, G, F, cx,
+    load_s, part_s, part_r, prm_s, prm_r, pair_s, pair_r,
+    near_s, near_r, far_s, far_r, z_s, z_r, c_s, c_r,
 ):
     pulse = lax.axis_index("pulse")
     ranged = lax.axis_index("range")
@@ -67,15 +69,21 @@
 
     barrier = pltpu.get_barrier_semaphore()
     pl.semaphore_signal(barrier, inc=1, device_id={"pulse": buddy}, device_id_type=MESH)
-    for k in range(1, 8):
+    pl.semaphore_signal(barrier, inc=1, device_id={"pulse": q6}, device_id_type=MESH)
+    for k in (1, 2, 6, 7):
         pl.semaphore_signal(barrier, inc=1, device_id={"pulse": z_peer(k)}, device_id_type=MESH)
     for k in range(1, 16):
         pl.semaphore_signal(barrier, inc=1, device_id={"range": r_peer(k)}, device_id_type=MESH)
 
     def fill(ref, level, source):
-        ref[0:4, :] = taps[level, source].astype(f32)
-        ref[4:8, :] = weights[level, source].astype(f32)
-        ref[8:9, :] = squint[level:level + 1, :]
+        tap = taps[level, source]
+        slope = squint[level:level + 1, :]
+        first = slope.astype(bf16).astype(f32)
+        second = (slope - first).astype(bf16).astype(f32)
+        third = slope - first - second
+        ref[...] = jnp.concatenate([
+            (tap % 256).astype(f32), (tap // 256).astype(f32), weights[level, source].astype(f32),
+            first, second, third, jnp.zeros_like(slope)], axis=0).astype(bf16)
 
     fill(snd.at[0], 1, 1)
     fill(snd.at[1], 2, 1)
@@ -88,8 +96,9 @@
     def build(m, slot):
         for nt in range(4):
             cols = slice(256 * nt, 256 * nt + 256)
-            places = [prm[m, tap:tap + 1, cols] for tap in range(4)]
-            scales = [prm[m, 4 + tap:5 + tap, cols].astype(bf16) for tap in range(4)]
+            rows = prm[m, :, cols].astype(f32)
+            places = [rows[tap:tap + 1] + 256.0 * rows[4 + tap:5 + tap] for tap in range(4)]
+            scales = [rows[8 + tap:9 + tap].astype(bf16) for tap in range(4)]
             for kb in range(4):
                 val = jnp.zeros((256, 256), bf16)
                 for tap in range(4):
@@ -100,7 +109,8 @@
     first_range = (ranged * COLS).astype(f32)
 
     def prepare_rotation(m):
-        slope = prm[m, 8:9, :]
+        rows = prm[m].astype(f32)
+        slope = rows[12:13] + rows[13:14] + rows[14:15]
         i8 = lax.broadcasted_iota(jnp.int32, (8, BEAMS), 0).astype(f32)
         c0, s0 = sincos(slope * ((i8 + first_range) * (1.0 / RANGES)))
         cf, sf = sincos(slope * (jnp.where(i8 < 1.0, 8.0, 128.0) * (1.0 / RANGES)))
@@ -141,41 +151,43 @@
     first_angle = BEAMS * (core + 8 * (z // 4))
 
     def table_base():
-        angle = lax.broadcasted_iota(jnp.int32, (16, BEAMS), 1) + first_angle
-        up = lax.broadcasted_iota(jnp.int32, (16, BEAMS), 0)
-        us[0], us[1] = sincos(((64 * up * angle) % ANGLES).astype(f32) * (1.0 / ANGLES))
+        angle = lax.broadcasted_iota(jnp.int32, (1, BEAMS), 1) + first_angle
+        rows = []
+        for step in STEPS:
+            for c in (core, other):
+                rows.append(angle * (64 * (((z + step) % 8) * 2 + c)))
+        us[0], us[1] = sincos((jnp.concatenate(rows, axis=0) % ANGLES).astype(f32) * (1.0 / ANGLES))
 
     def table(k):
         a8 = lax.broadcasted_iota(jnp.int32, (8, BEAMS), 1) + first_angle
         v8 = 8 * lax.broadcasted_iota(jnp.int32, (8, BEAMS), 0) + k
         vc, vs = sincos(((v8 * a8) % ANGLES).astype(f32) * (1.0 / ANGLES))
-        for pair in range(8):
+        for q in range(8):
             cs = []
             ss = []
-            for u in (2 * pair, 2 * pair + 1):
+            for u in (2 * q, 2 * q + 1):
                 uc = us[0, u:u + 1, :]
                 un = us[1, u:u + 1, :]
                 cs.append(uc * vc - un * vs)
                 ss.append(un * vc + uc * vs)
-            tab[k, 16 * pair:16 * pair + 16, :] = jnp.concatenate(cs, axis=0).astype(bf16)
-            tab[k, 128 + 16 * pair:144 + 16 * pair, :] = jnp.concatenate(ss, axis=0).astype(bf16)
+            at_c, at_s = (16 * q, 48 + 16 * q) if q < 3 else (48 + 16 * q, 128 + 16 * q)
+            tab[k, at_c:at_c + 16, :] = jnp.concatenate(cs, axis=0).astype(bf16)
+            tab[k, at_s:at_s + 16, :] = jnp.concatenate(ss, axis=0).astype(bf16)
 
     build(0, 0)
-    prepare_rotation(0)
-    table_base()
 
     load.wait()
     for t in range(2):
         dT[0, t * COLS:(t + 1) * COLS, :] = data[t].T
 
-    pl.semaphore_wait(barrier, 23)
+    pl.semaphore_wait(barrier, 21)
 
     part = pltpu.make_async_remote_copy(
         dT.at[0], dT.at[1], part_s, part_r, device_id={"pulse": buddy}, device_id_type=MESH)
     part.start()
     prm_copies = []
     for n, (src, slot, target) in enumerate((
-        (snd.at[1], 7, q6), (snd.at[1], 5, q4), (snd.at[0], 3, q2), (prm.at[4], 6, q2))):
+        (snd.at[0], 3, q2), (snd.at[1], 5, q4), (prm.at[4], 6, q2), (snd.at[1], 7, q6))):
         copy = pltpu.make_async_remote_copy(
             src, prm.at[slot], prm_s.at[n], prm_r.at[n],
             device_id={"pulse": target}, device_id_type=MESH)
@@ -184,17 +196,18 @@
 
     acc[0] = jnp.dot(dT[0], W[0], preferred_element_type=f32)
     build(1, 1)
+    prepare_rotation(0)
+    table_base()
     prepare_rotation(2)
     table(0)
     part.wait()
     acc[1] = jnp.dot(dT[1], W[1], preferred_element_type=f32) + acc[0]
     build(2, 0)
     table(1)
-    for copy in prm_copies:
-        copy.wait()
     rotate_all(acc.at[1], 0, S1, bf16)
 
     acc[0] = jnp.dot(S1[...], W[0], preferred_element_type=f32)
+    prm_copies[0].wait()
     build(3, 1)
     prepare_rotation(3)
     table(2)
@@ -214,18 +227,21 @@
         return at0 + 2 * at1
 
     acc[0] = jnp.dot(U[0], W[0], preferred_element_type=f32)
+    prm_copies[1].wait()
     build(5, 1)
     rotate_all(acc.at[1], 3, U.at[1], bf16)
     prepare_rotation(5)
     table(4)
 
     acc[1] = jnp.dot(U[0], W[1], preferred_element_type=f32)
+    prm_copies[2].wait()
     build(6, 0)
     rotate_all(acc.at[0], 4, X.at[slot_of(0)], f32)
     prepare_rotation(6)
     table(5)
 
     acc[0] = jnp.dot(U[1], W[0], preferred_element_type=f32)
+    prm_copies[3].wait()
     build(7, 1)
     rotate_all(acc.at[1], 5, X.at[slot_of(2)], f32)
     prepare_rotation(7)
@@ -239,7 +255,7 @@
     root = math.sqrt(0.5)
 
     def combine(half, nt):
-        cols = pl.ds(nt * 256, 256) if isinstance(nt, int) else pl.ds(pl.multiple_of(nt * 256, 256), 256)
+        cols = slice(256 * nt, 256 * nt + 256)
         for step in range(8):
             top = slice(128 * half + 16 * step, 128 * half + 16 * step + 16)
             low = slice(256 + 128 * half + 16 * step, 272 + 128 * half + 16 * step)
@@ -273,46 +289,72 @@
 
     scale = ANGLES ** (-0.5)
 
-    def spectrum(half, beside):
-        def body(kk, carry):
+    def spectrum(half, group, beside):
+        lo, hi, size = ((0, 3, 48), (3, 8, 80))[group]
+        first = 96 * group
+        for kk in range(4):
             res = []
             ims = []
-            for e in range(2):
+            for k in (2 * kk, 2 * kk + 1):
                 both = lax.dot_general(
-                    tab[2 * kk + e], Y[half, 2 * kk + e], NT, preferred_element_type=f32)
-                res.append((both[:128, :128] + both[128:, 128:]) * scale)
-                ims.append((both[:128, 128:] - both[128:, :128]) * scale)
+                    tab[k, first:first + 2 * size, :], Y[half, k], NT, preferred_element_type=f32)
+                res.append((both[:size, :128] + both[size:, 128:]) * scale)
+                ims.append((both[:size, 128:] - both[size:, :128]) * scale)
             for t, parts in enumerate((res, ims)):
-                val = jnp.concatenate([p.reshape(16, 8, 128) for p in parts], axis=1)
-                val = val.reshape(8, 2, 16, 128)
-                for c in range(2):
-                    fst[half, c, :, kk, t] = val[:, c]
-                    stg[half, c, :, kk, t] = val[:, c].astype(bf16)
+                val = jnp.concatenate([p.reshape(size // 8, 8, 128) for p in parts], axis=1)
+                val = val.reshape(hi - lo, 2, 16, 128)
+                fst[half, lo:hi, kk, t] = val[:, 0]
+                stg[half, lo:hi, kk, t] = val[:, 1].astype(bf16)
             if beside is not None:
                 combine(beside, kk)
-            return carry
-
-        lax.fori_loop(0, 4, body, 0)
-
-    def pair_copy(half):
+
+    def to(src, dst, send, recv, target):
         return pltpu.make_async_remote_copy(
-            stg.at[half, other], prx.at[half], pair_s.at[half], pair_r.at[half],
-            device_id={"pulse": buddy}, device_id_type=MESH)
-
-    order = (4, 3, 5, 2, 6, 1, 7)
-
-    def z_copy(half, k):
-        return pltpu.make_async_remote_copy(
-            zsn.at[half, (z + k) % 8], zrx.at[half, k - 1],
-            z_s.at[half, k - 1], z_r.at[half, k - 1],
-            device_id={"pulse": z_peer(k)}, device_id_type=MESH)
+            src, dst, send, recv, device_id={"pulse": target}, device_id_type=MESH)
+
+    def pair(half, group):
+        lo, size = ((0, 3), (3, 5))[group]
+        return to(stg.at[half, pl.ds(lo, size)], prx.at[half, pl.ds(lo, size)],
+                  pair_s.at[half, group], pair_r.at[half, group], buddy)
+
+    def near_copy(half, n):
+        return to(zsn.at[half, 1 + n], near.at[half, n],
+                  near_s.at[half, n], near_r.at[half, n], z_peer((1, 7)[n]))
+
+    def far_copy(half, n):
+        return to(zsn.at[half, 0, :, n], far.at[half, n],
+                  far_s.at[half, n], far_r.at[half, n], z_peer((2, 6)[n]))
+
+    def z_copy(half, n):
+        return to(zsn.at[half, (5, 6, 4, 7)[n]], zrx.at[half, n],
+                  z_s.at[half, n], z_r.at[half, n], z_peer((2, 6, 1, 7)[n]))
+
+    def relay(half):
+        pair(half, 0).wait()
+        for q in range(3):
+            zsn[half, q] = (fst[half, q] + prx[half, q].astype(f32)).astype(bf16)
+        for n in range(2):
+            far_copy(half, n).start()
+        for n in range(2):
+            near_copy(half, n).start()
 
     def scatter(half):
-        pair_copy(half).wait()
-        for d in range(8):
-            zsn[half, d] = (fst[half, core, d] + prx[half, d].astype(f32)).astype(bf16)
-        for k in order:
-            z_copy(half, k).start()
+        pair(half, 1).wait()
+        for n in (2, 3):
+            q = (5, 6, 4, 7)[n]
+            zsn[half, q] = (fst[half, q] + prx[half, q].astype(f32)).astype(bf16)
+            z_copy(half, n).start()
+        fst[half, 3] = fst[half, 3] + prx[half, 3].astype(f32)
+        for n in (0, 1):
+            far_copy(half, n).wait()
+            near_copy(half, n).wait()
+            q = 5 + n
+            for t in range(2):
+                both = fst[half, q, :, t] + prx[half, q, :, t].astype(f32) + near[half, n, :, t].astype(f32)
+                if t == n:
+                    both = both + far[half, n].astype(f32)
+                zsn[half, q, :, t] = both.astype(bf16)
+            z_copy(half, n).start()
 
     last(0)
     rotate_all(acc.at[0], 6, X.at[slot_of(1)], f32)
@@ -322,18 +364,24 @@
     for nt in range(4):
         combine(0, nt)
     rotate(acc.at[1], 7, 1, X.at[slot_of(3)], f32, 256, 384)
-    spectrum(0, 1)
-    pair_copy(0).start()
+    spectrum(0, 0, 1)
+    pair(0, 0).start()
+    spectrum(1, 0, None)
+    pair(1, 0).start()
+    relay(0)
+    spectrum(0, 1, None)
+    pair(0, 1).start()
+    relay(1)
+    spectrum(1, 1, None)
+    pair(1, 1).start()
     scatter(0)
-    spectrum(1, None)
-    pair_copy(1).start()
     scatter(1)
 
     for half in range(2):
-        total = fst[half, core, z] + prx[half, z].astype(f32)
-        for k in order:
-            z_copy(half, k).wait()
-            total = total + zrx[half, k - 1].astype(f32)
+        total = fst[half, 3]
+        for n in (2, 3, 0, 1):
+            z_copy(half, n).wait()
+            total = total + zrx[half, n].astype(f32)
         for kk in range(4):
             for t in range(2):
                 G[64 * t + 16 * kk:64 * t + 16 * kk + 16, 128 * half:128 * half + 128] = total[kk, t]
@@ -402,8 +450,8 @@
         scratch_shapes=[
             pltpu.VMEM((2, BEAMS, COLS), bf16),
             pltpu.VMEM((2, 512, BEAMS), bf16),
-            pltpu.VMEM((8, 16, BEAMS), f32),
-            pltpu.VMEM((2, 16, BEAMS), f32),
+            pltpu.VMEM((8, 16, BEAMS), bf16),
+            pltpu.VMEM((2, 16, BEAMS), bf16),
             pltpu.VMEM((2, BEAMS, BEAMS), bf16),
             pltpu.VMEM((256, 256), bf16),
             pltpu.VMEM((8, 2, 2, 8, BEAMS), f32),
@@ -415,18 +463,22 @@
             pltpu.VMEM((2, 8, 256, BEAMS), bf16),
             pltpu.VMEM((2, 16, BEAMS), f32),
             pltpu.VMEM((8, 256, BEAMS), bf16),
-            pltpu.VMEM((2, 2, 8, 4, 2, 16, 128), f32),
-            pltpu.VMEM((2, 2, 8, 4, 2, 16, 128), bf16),
+            pltpu.VMEM((2, 8, 4, 2, 16, 128), f32),
             pltpu.VMEM((2, 8, 4, 2, 16, 128), bf16),
             pltpu.VMEM((2, 8, 4, 2, 16, 128), bf16),
-            pltpu.VMEM((2, 7, 4, 2, 16, 128), bf16),
+            pltpu.VMEM((2, 8, 4, 2, 16, 128), bf16),
+            pltpu.VMEM((2, 2, 4, 2, 16, 128), bf16),
+            pltpu.VMEM((2, 2, 4, 16, 128), bf16),
+            pltpu.VMEM((2, 4, 4, 2, 16, 128), bf16),
             pltpu.VMEM((128, COLS), f32),
             pltpu.VMEM((2, 2, 64, 128), f32),
             pltpu.VMEM((16, 32, 128), f32),
             dma, dma, dma,
             dma((4,)), dma((4,)),
-            dma((2,)), dma((2,)),
-            dma((2, 7)), dma((2, 7)),
+            dma((2, 2)), dma((2, 2)),
+            dma((2, 2)), dma((2, 2)),
+            dma((2, 2)), dma((2, 2)),
+            dma((2, 4)), dma((2, 4)),
             dma((15,)), dma((15,)),
         ],
         compiler_params=pltpu.CompilerParams(

time: 58.4 us -> 49.7 us (0.85)
  Pallas kernels: 56.7 us -> 48 us
    pallas_call x1, Pallas kernels: 56.7 us -> 48 us  [per_device(): pl.pallas_call(kernel, out_shape=jax.ShapeDtypeStruct((2, BLOCK, COLS), f...]
where the time goes in v3:
time: 49.7 us; the launch traced here: 49.5 us
  Pallas kernels  48 us (97%)
  local copies, waits for them, and re-layouts  1.57 us (3%)
    pallas_call x1, Pallas kernels, per_device(): pl.pallas_call(kernel, out_shape=jax.ShapeDtypeStruct((2, BLOCK, COLS), f...  48 us
    unnamed x1, local copies, waits for them, and re-layouts  1.57 us

profile of v3, /device:TPU:1, one launch (start us, length us, event | category | flops | bytes accessed | tf_op | source)
XLA Modules:
  0.0 49.5 jit_solution(17978777747169892998)
XLA Ops:
  0.0 48.0 %shard_map.46 = f32[2,64,256]{2,1,0:T(8,128)} custom-call(bf16[2,1024,256]{2,1,0:T(8,128)(2,1)} %data_hbm.1, s32[3,2,4,1024]{3,2,1,0:T(4,128)} %taps.1, bf16[3,2,4,1024]{3,2,1,0:T(4,128)(2,1)} %weights.1, f32[3,1024]{1,0:T(4,128)} %squint.1), custom_call_target="tpu_custom_call" | custom-call | tf_op jit(solution)/shard_map/pallas_call | solution.py:445
  48.0 1.6 %copy.6 = f32[2,64,256]{2,1,0:T(8,128)} copy(f32[2,64,256]{2,1,0:T(8,128)} %shard_map.46) | data formatting | bytes 262144

commit v4 on v3

--- a/solution.py
+++ b/solution.py
@@ -289,22 +289,25 @@
 
     scale = ANGLES ** (-0.5)
 
-    def spectrum(half, group, beside):
-        lo, hi, size = ((0, 3, 48), (3, 8, 80))[group]
-        first = 96 * group
-        for kk in range(4):
-            res = []
-            ims = []
-            for k in (2 * kk, 2 * kk + 1):
-                both = lax.dot_general(
-                    tab[k, first:first + 2 * size, :], Y[half, k], NT, preferred_element_type=f32)
-                res.append((both[:size, :128] + both[size:, 128:]) * scale)
-                ims.append((both[:size, 128:] - both[size:, :128]) * scale)
-            for t, parts in enumerate((res, ims)):
-                val = jnp.concatenate([p.reshape(size // 8, 8, 128) for p in parts], axis=1)
-                val = val.reshape(hi - lo, 2, 16, 128)
-                fst[half, lo:hi, kk, t] = val[:, 0]
-                stg[half, lo:hi, kk, t] = val[:, 1].astype(bf16)
+    def spectrum(half, groups, beside, steps):
+        first = 96 * groups[0]
+        end = 96 if groups[-1] == 0 else 256
+        for kk in steps:
+            boths = [
+                lax.dot_general(tab[k, first:end, :], Y[half, k], NT, preferred_element_type=f32)
+                for k in (2 * kk, 2 * kk + 1)]
+            for group in groups:
+                lo, hi, size = ((0, 3, 48), (3, 8, 80))[group]
+                top = 96 * group - first
+                cosines = [both[top:top + size] for both in boths]
+                sines = [both[top + size:top + 2 * size] for both in boths]
+                res = [(c[:, :128] + n[:, 128:]) * scale for c, n in zip(cosines, sines)]
+                ims = [(c[:, 128:] - n[:, :128]) * scale for c, n in zip(cosines, sines)]
+                for t, parts in enumerate((res, ims)):
+                    val = jnp.concatenate([p.reshape(size // 8, 8, 128) for p in parts], axis=1)
+                    val = val.reshape(hi - lo, 2, 16, 128)
+                    fst[half, lo:hi, kk, t] = val[:, 0]
+                    stg[half, lo:hi, kk, t] = val[:, 1].astype(bf16)
             if beside is not None:
                 combine(beside, kk)
 
@@ -364,15 +367,15 @@
     for nt in range(4):
         combine(0, nt)
     rotate(acc.at[1], 7, 1, X.at[slot_of(3)], f32, 256, 384)
-    spectrum(0, 0, 1)
+    spectrum(0, (0, 1), 1, range(4))
     pair(0, 0).start()
-    spectrum(1, 0, None)
+    pair(0, 1).start()
+    spectrum(1, (0,), None, range(4))
     pair(1, 0).start()
     relay(0)
-    spectrum(0, 1, None)
-    pair(0, 1).start()
+    spectrum(1, (1,), None, range(2))
     relay(1)
-    spectrum(1, 1, None)
+    spectrum(1, (1,), None, range(2, 4))
     pair(1, 1).start()
     scatter(0)
     scatter(1)

time: 49.7 us -> 49.1 us (0.988)
  Pallas kernels: 48 us -> 47.3 us
    pallas_call x1, Pallas kernels: 48 us -> 47.3 us  [per_device(): pl.pallas_call(kernel, out_shape=jax.ShapeDtypeStruct((2, BLOCK, COLS), f...]
where the time goes in v4:
time: 49.1 us; the launch traced here: 48.9 us
  Pallas kernels  47.3 us (96%)
  local copies, waits for them, and re-layouts  1.57 us (3%)
    pallas_call x1, Pallas kernels, per_device(): pl.pallas_call(kernel, out_shape=jax.ShapeDtypeStruct((2, BLOCK, COLS), f...  47.3 us
    unnamed x1, local copies, waits for them, and re-layouts  1.57 us

profile of v4, /device:TPU:1, one launch (start us, length us, event | category | flops | bytes accessed | tf_op | source)
XLA Modules:
  0.0 48.9 jit_solution(1672058003017095611)
XLA Ops:
  0.0 47.3 %shard_map.46 = f32[2,64,256]{2,1,0:T(8,128)} custom-call(bf16[2,1024,256]{2,1,0:T(8,128)(2,1)} %data_hbm.1, s32[3,2,4,1024]{3,2,1,0:T(4,128)} %taps.1, bf16[3,2,4,1024]{3,2,1,0:T(4,128)(2,1)} %weights.1, f32[3,1024]{1,0:T(4,128)} %squint.1), custom_call_target="tpu_custom_call" | custom-call | tf_op jit(solution)/shard_map/pallas_call | solution.py:448
  47.3 1.6 %copy.6 = f32[2,64,256]{2,1,0:T(8,128)} copy(f32[2,64,256]{2,1,0:T(8,128)} %shard_map.46) | data formatting | bytes 262144

commit v5 on v4

--- a/solution.py
+++ b/solution.py
@@ -341,13 +341,15 @@
         for n in range(2):
             near_copy(half, n).start()
 
-    def scatter(half):
+    def direct(half):
         pair(half, 1).wait()
         for n in (2, 3):
             q = (5, 6, 4, 7)[n]
             zsn[half, q] = (fst[half, q] + prx[half, q].astype(f32)).astype(bf16)
             z_copy(half, n).start()
         fst[half, 3] = fst[half, 3] + prx[half, 3].astype(f32)
+
+    def scatter(half):
         for n in (0, 1):
             far_copy(half, n).wait()
             near_copy(half, n).wait()
@@ -373,11 +375,13 @@
     spectrum(1, (0,), None, range(4))
     pair(1, 0).start()
     relay(0)
+    direct(0)
     spectrum(1, (1,), None, range(2))
     relay(1)
     spectrum(1, (1,), None, range(2, 4))
     pair(1, 1).start()
     scatter(0)
+    direct(1)
     scatter(1)
 
     for half in range(2):

time: 49.1 us -> 49 us (level)
  Pallas kernels: 47.3 us -> 46.8 us
    pallas_call x1, Pallas kernels: 47.3 us -> 46.8 us  [per_device(): pl.pallas_call(kernel, out_shape=jax.ShapeDtypeStruct((2, BLOCK, COLS), f...]
where the time goes in v5:
time: 49 us; the launch traced here: 48.4 us
  Pallas kernels  46.8 us (96%)
  local copies, waits for them, and re-layouts  1.57 us (3%)
    pallas_call x1, Pallas kernels, per_device(): pl.pallas_call(kernel, out_shape=jax.ShapeDtypeStruct((2, BLOCK, COLS), f...  46.8 us
    unnamed x1, local copies, waits for them, and re-layouts  1.57 us

profile of v5, /device:TPU:1, one launch (start us, length us, event | category | flops | bytes accessed | tf_op | source)
XLA Modules:
  0.0 48.4 jit_solution(6705803210099702836)
XLA Ops:
  0.0 46.8 %shard_map.46 = f32[2,64,256]{2,1,0:T(8,128)} custom-call(bf16[2,1024,256]{2,1,0:T(8,128)(2,1)} %data_hbm.1, s32[3,2,4,1024]{3,2,1,0:T(4,128)} %taps.1, bf16[3,2,4,1024]{3,2,1,0:T(4,128)(2,1)} %weights.1, f32[3,1024]{1,0:T(4,128)} %squint.1), custom_call_target="tpu_custom_call" | custom-call | tf_op jit(solution)/shard_map/pallas_call | solution.py:452
  46.8 1.6 %copy.6 = f32[2,64,256]{2,1,0:T(8,128)} copy(f32[2,64,256]{2,1,0:T(8,128)} %shard_map.46) | data formatting | bytes 262144
